TPU v7x, 128 devices: a whole 4x4x4 slice. The times are simulated.
128 devices in a mesh: row: 16 (over z_hi, y, core), col: 8 (over x, z_lo).
Axes of the slice: x: 4, y: 4, z: 4 (z_hi: 2, z_lo: 2; z = z_hi * 2 + z_lo), core: 2. Of those that a mesh axis runs over, the one named last changes fastest.
Arguments:
- word_topic: bfloat16 [131072, 128], P(('row', 'col')), may hold values from 0.25 to 4
- topic_weight: float32 [128], replicated, may hold values from 0.1 to 10
- tile_blocks: int32 [16, 8, 64, 2], P('row', 'col'), may hold values from 0 to 63, as said below
- tile_live: int32 [16, 8], P('row', 'col'), may hold values from 16 to 64, as said below
- pair_counts: int32 [16, 8, 64, 256, 256], P('row', 'col'), may hold values from 0 to 63
Outputs:
- next_word_topic: bfloat16 [131072, 128], P(('row', 'col'))
- next_topic_weight: float32 [128], replicated
Inputs may be any that keep to these rules, and one draw needn't show every extreme that they name: `tile_blocks`: each entry pair is (a word block among the device's 32 blocks of first words, a word block among its 64 blocks of second words); the slots of one device name distinct tiles. `tile_live`: slots at or beyond a device's count hold no tile; some device fills all slots.
All inputs are finite; a program needn't handle non-finite values.
Results may differ from a plain program's by a relative error of at most 0.0049.
Values may be sent and summed in bfloat16 or wider, within the bound.
No kernel may reach another device: no remote copies, remote signals or barrier semaphores. Data moves between devices by JAX's collectives and lax.ppermute only.
A program may use at most 128 MiB of HBM per device.

v0:
```python
from functools import partial
import jax
import jax.numpy as jnp
from jax import lax
from jax.sharding import PartitionSpec as P

V = 131072
K = 128
BLK = 256
ITERS = 2


def group_step(
    left_blocks, right_blocks, blocks, tiles_all, live, want_row, want_col, group, carry
):
    tile_group = 8
    start = group * tile_group
    row_ids = lax.dynamic_slice_in_dim(blocks[:, 0], start, tile_group)
    col_ids = lax.dynamic_slice_in_dim(blocks[:, 1], start, tile_group)
    tiles = lax.dynamic_slice_in_dim(tiles_all, start, tile_group, 0)
    alive = start + jnp.arange(tile_group, dtype=jnp.int32) < live
    left = left_blocks[row_ids]
    right = right_blocks[col_ids]
    denoms = jnp.einsum("gak,gbk->gab", left, right, preferred_element_type=jnp.float32)
    ratio = jnp.where(alive[:, None, None], tiles.astype(jnp.float32) / denoms, 0.0).astype(
        jnp.bfloat16
    )
    results = []
    place = 0
    row_part = jnp.einsum("gab,gbk->gak", ratio, right, preferred_element_type=jnp.float32)
    results.append(carry[place].at[row_ids].add(row_part))
    place = place + 1
    col_part = jnp.einsum("gab,gak->gbk", ratio, left, preferred_element_type=jnp.float32)
    results.append(carry[place].at[col_ids].add(col_part))
    return tuple(results)


def sweep(left_blocks, right_blocks, blocks, tiles_all, live):
    starts = []
    starts.append(jnp.zeros(left_blocks.shape, jnp.float32))
    starts.append(jnp.zeros(right_blocks.shape, jnp.float32))
    stepper = partial(group_step, left_blocks, right_blocks, blocks, tiles_all, live, True, True)
    turns = (live + 7) // 8
    return lax.fori_loop(0, turns, stepper, tuple(starts))


def local(word_topic, topic_weight, tile_blocks, tile_live, pair_counts):
    blocks = tile_blocks[0, 0]
    live = tile_live[0, 0]
    tiles_all = pair_counts[0, 0]
    weights = word_topic
    shares = topic_weight
    for step in range(ITERS):
        row_phi = lax.all_gather(weights, "col", axis=0, tiled=True)
        col_phi = lax.all_gather(weights, "row", axis=0, tiled=True)
        scaled = (row_phi.astype(jnp.float32) * shares).astype(jnp.bfloat16)
        left_blocks = scaled.reshape(-1, BLK, K)
        right_blocks = col_phi.reshape(-1, BLK, K)
        row_acc, col_acc = sweep(left_blocks, right_blocks, blocks, tiles_all, live)
        row_terms = row_acc.reshape(-1, K)
        col_terms = col_acc.reshape(-1, K)
        row_sum = lax.psum_scatter(row_terms, "col", scatter_dimension=0, tiled=True)
        col_sum = lax.psum_scatter(col_terms, "row", scatter_dimension=0, tiled=True)
        expected = weights.astype(jnp.float32) * (shares * row_sum + col_sum)
        totals = lax.psum(jnp.sum(expected, axis=0), ("row", "col"))
        weights = (V * expected / totals).astype(jnp.bfloat16)
        shares = K * totals / jnp.sum(totals)
    return (weights, shares)


def solution(mesh):
    in_specs = (
        P(("row", "col"), None),
        P(),
        P("row", "col", None, None),
        P("row", "col"),
        P("row", "col", None, None, None),
    )
    out_specs = (P(("row", "col"), None), P())
    return jax.shard_map(local, mesh=mesh, in_specs=in_specs, out_specs=out_specs, check_vma=False)
```

profile of v0, /device:TPU:1, one launch (start us, length us, event | category | flops | bytes accessed | tf_op | source)
XLA Modules:
  0.0 1029.4 jit_solution(16607636807630387287)
XLA Ops:
  9.4 52.8 %all-gather.5.cloned.1.call-done = bf16[8192,128]{1,0:T(8,128)(2,1)} async-done(((bf16[1024,128]{1,0:T(8,128)(2,1)}), bf16[8192,128]{1,0:T(8,128)(2,1)}) %all-gather.5.cloned.1.call-update) | async-done | bytes 2097168 | tf_op jit(solution)/shard_map/all_gather | solution.py:54
  62.1 3.3 multiply_convert_fusion.1
  65.5 57.8 %all-gather.7.cloned.1.call-done = bf16[16384,128]{1,0:T(8,128)(2,1)} async-done(((bf16[1024,128]{1,0:T(8,128)(2,1)}), bf16[16384,128]{1,0:T(8,128)(2,1)}) %all-gather.7.cloned.1.call-update) | async-done | bytes 4194320 | tf_op jit(solution)/shard_map/all_gather | solution.py:55
  123.3 4.2 broadcast.60.clone
  130.0 108.6 %while.24 = (s32[]{:T(128)}, f32[32,256,128]{2,1,0:T(8,128)}, f32[64,256,128]{2,1,0:T(8,128)}, s32[]{:T(128)}, s32[64,2]{0,1:T(2,128)S(1)}, /*index=5*/s32[]{:T(...) while((s32[]{:T(128)}, f32[32,256,128]{2,1,0:T(8,128)}, ...), condition=%wide.region_3.4_spmd, body=%wide.region_0.3_spmd.sunk | while | flops 405276736 | bytes 17835532 | solution.py:44
  138.4 3.4 scatter_fusion.1
  142.3 3.3 scatter_fusion
  154.1 3.3 scatter_fusion.1
  173.3 3.3 scatter_fusion
  185.0 3.4 scatter_fusion.1
  216.0 3.4 scatter_fusion.1
  231.5 3.4 scatter_fusion.1
  235.3 3.4 scatter_fusion
  239.3 103.5 %reduce-scatter.5.cloned.1.call-done = f32[1024,128]{1,0:T(8,128)} async-done(((f32[8192,128]{1,0:T(8,128)}), f32[1024,128]{1,0:T(8,128)}) %reduce-scatter.5.cloned.1.call-update) | async-done | bytes 524304 | tf_op jit(solution)/shard_map/reduce_scatter | solution.py:62
  342.8 106.7 %reduce-scatter.7.cloned.1.call-done = f32[1024,128]{1,0:T(8,128)} async-done(((f32[16384,128]{1,0:T(8,128)}), f32[1024,128]{1,0:T(8,128)}) %reduce-scatter.7.cloned.1.call-update) | async-done | bytes 524304 | tf_op jit(solution)/shard_map/reduce_scatter | solution.py:63
  450.9 65.3 %psum.14 = f32[128]{0:T(128)S(1)} all-reduce(f32[128]{0:T(128)S(1)} %fusion.4), channel_id=1, replica_groups=mesh['row'=16,'col'=8] {'row','col'}, use_global_device_ids=true, to_apply=%region_7.8 | all-reduce | flops 128 | bytes 1024 | tf_op jit(solution)/shard_map/psum | solution.py:65
  520.1 43.9 %all-gather.9.cloned.1.call-done = bf16[8192,128]{1,0:T(8,128)(2,1)} async-done(((bf16[1024,128]{1,0:T(8,128)(2,1)}), bf16[8192,128]{1,0:T(8,128)(2,1)}) %all-gather.9.cloned.1.call-update) | async-done | bytes 2097168 | tf_op jit(solution)/shard_map/all_gather | solution.py:54
  564.1 3.3 multiply_convert_fusion
  567.4 58.3 %all-gather.11.cloned.1.call-done = bf16[16384,128]{1,0:T(8,128)(2,1)} async-done(((bf16[1024,128]{1,0:T(8,128)(2,1)}), bf16[16384,128]{1,0:T(8,128)(2,1)}) %all-gather.11.cloned.1.call-update) | async-done | bytes 4194320 | tf_op jit(solution)/shard_map/all_gather | solution.py:55
  625.7 4.2 broadcast.60
  632.4 108.6 %while.25 = (s32[]{:T(128)}, f32[32,256,128]{2,1,0:T(8,128)}, f32[64,256,128]{2,1,0:T(8,128)}, s32[]{:T(128)}, s32[64,2]{0,1:T(2,128)S(1)}, /*index=5*/s32[]{:T(...) while((s32[]{:T(128)}, f32[32,256,128]{2,1,0:T(8,128)}, ...), condition=%wide.region_12.13_spmd, body=%wide.region_9.12_spmd.sunk | while | flops 405276736 | bytes 17835532 | solution.py:44
  640.8 3.4 scatter_fusion.3
  644.6 3.3 scatter_fusion.2
  656.4 3.3 scatter_fusion.3
  675.6 3.3 scatter_fusion.2
  687.4 3.4 scatter_fusion.3
  718.4 3.4 scatter_fusion.3
  733.9 3.4 scatter_fusion.3
  737.7 3.4 scatter_fusion.2
  741.8 103.4 %reduce-scatter.9.cloned.1.call-done = f32[1024,128]{1,0:T(8,128)} async-done(((f32[8192,128]{1,0:T(8,128)}), f32[1024,128]{1,0:T(8,128)}) %reduce-scatter.9.cloned.1.call-update) | async-done | bytes 524304 | tf_op jit(solution)/shard_map/reduce_scatter | solution.py:62
  845.2 106.7 %reduce-scatter.11.cloned.1.call-done = f32[1024,128]{1,0:T(8,128)} async-done(((f32[16384,128]{1,0:T(8,128)}), f32[1024,128]{1,0:T(8,128)}) %reduce-scatter.11.cloned.1.call-update) | async-done | bytes 524304 | tf_op jit(solution)/shard_map/reduce_scatter | solution.py:63
  953.2 65.5 %psum.15 = f32[128]{0:T(128)S(1)} all-reduce(f32[128]{0:T(128)S(1)} %fusion.5), channel_id=1, replica_groups=mesh['row'=16,'col'=8] {'row','col'}, use_global_device_ids=true, to_apply=%region_16.17 | all-reduce | flops 128 | bytes 1024 | tf_op jit(solution)/shard_map/psum | solution.py:65
  (186 shorter events, 180.9 us)
Async XLA Ops:
  7.2 55.0 %all-gather.5.cloned.1.call-start = ((), (), s32[]{:S(2)}) async-start(), calls=%async_computation.4 | async-start | bytes 2359296 | tf_op jit(solution)/shard_map/all_gather | solution.py:54
  7.9 115.4 %all-gather.7.cloned.1.call-start = ((), (), s32[]{:S(2)}) async-start(), calls=%async_computation.5 | async-start | bytes 4456448 | tf_op jit(solution)/shard_map/all_gather | solution.py:55
  8.6 334.2 %reduce-scatter.5.cloned.1.call-start = ((), (), s32[]{:S(2)}) async-start(), calls=%async_computation.6 | async-start | bytes 4718592 | tf_op jit(solution)/shard_map/reduce_scatter | solution.py:62
  127.6 2.5 copy-start.2
  238.7 210.9 %reduce-scatter.7.cloned.1.call-start = ((), (), s32[]{:S(2)}) async-start(), calls=%async_computation.7 | async-start | bytes 8912896 | tf_op jit(solution)/shard_map/reduce_scatter | solution.py:63
  238.7 210.8 %copy-start.1 = (bf16[1024,128]{1,0:T(8,128)(2,1)S(1)}, bf16[1024,128]{1,0:T(8,128)(2,1)}, u32[]{:S(2)}) copy-start(bf16[1024,128]{1,0:T(8,128)(2,1)} %param.9) | copy-start | bytes 786436
  238.7 210.8 %copy-start.3 = (f32[128]{0:T(128)S(1)}, f32[128]{0:T(128)}, u32[]{:S(2)}) copy-start(f32[128]{0:T(128)} %param.10) | copy-start | bytes 1540
  239.3 324.8 %all-gather.9.cloned.1.call-start = ((), (), s32[]{:S(2)}) async-start(), calls=%async_computation.8 | async-start | bytes 2359296 | tf_op jit(solution)/shard_map/all_gather | solution.py:54
  518.2 107.5 %all-gather.11.cloned.1.call-start = ((), (), s32[]{:S(2)}) async-start(), calls=%async_computation.9 | async-start | bytes 4456448 | tf_op jit(solution)/shard_map/all_gather | solution.py:55
  518.8 326.4 %reduce-scatter.9.cloned.1.call-start = ((), (), s32[]{:S(2)}) async-start(), calls=%async_computation.10 | async-start | bytes 4718592 | tf_op jit(solution)/shard_map/reduce_scatter | solution.py:62
  741.0 210.8 %reduce-scatter.11.cloned.1.call-start = ((), (), s32[]{:S(2)}) async-start(), calls=%async_computation.11 | async-start | bytes 8912896 | tf_op jit(solution)/shard_map/reduce_scatter | solution.py:63
  741.1 210.8 %copy-start = (bf16[1024,128]{1,0:T(8,128)(2,1)S(1)}, bf16[1024,128]{1,0:T(8,128)(2,1)}, u32[]{:S(2)}) copy-start(bf16[1024,128]{1,0:T(8,128)(2,1)} %divide_convert_fusion.1) | copy-start | bytes 786436
Sparse Core Ops, SparseCore 0:
  9.6 52.4 all-gather.4
  64.6 58.7 all-gather.6
  238.8 103.9 reduce-scatter.4
  347.0 102.4 reduce-scatter.6
  518.3 45.6 all-gather.8
  566.9 58.7 all-gather.10
  741.2 103.9 reduce-scatter.8
  849.5 102.2 reduce-scatter.10
where the time goes:
time: 1030 us
  waiting for transfers between devices  636 us (62%)
  blocking collectives  131 us (13%)
  other arithmetic  120 us (12%)
  local copies, waits for them, and re-layouts  84.5 us (8%)
  matrix products  41.8 us (4%)
  between operations  14.8 us (1%)
    reduce_scatter x2, waiting for transfers between devices, local(): lax.psum_scatter(col_terms, 'row', scatter_dimension=0, tiled=True)  213 us
    reduce_scatter x2, waiting for transfers between devices, local(): lax.psum_scatter(row_terms, 'col', scatter_dimension=0, tiled=True)  207 us
    psum x2, blocking collectives, local(): totals = lax.psum(jnp.sum(expected, axis=0), ('row', 'col'))  131 us
    all_gather x2, waiting for transfers between devices, local(): col_phi = lax.all_gather(weights, 'row', axis=0, tiled=True)  116 us
    all_gather x2, waiting for transfers between devices, local(): row_phi = lax.all_gather(weights, 'col', axis=0, tiled=True)  96.7 us
    scatter-add x14, other arithmetic, group_step(): results.append(carry[place].at[col_ids].add(col_part))  46.9 us
    scatter-add x14, other arithmetic, group_step(): results.append(carry[place].at[row_ids].add(row_part))  46.4 us
    gather x14, local copies, waits for them, and re-layouts, group_step(): right = right_blocks[col_ids]  39.7 us
  transfers between devices with their start and end apart: 8, of which 8 were waited for; matrix products, arithmetic and copies ran while one was open for 1% of the time, Pallas kernels for 0%

commit v1 on v0

--- a/solution.py
+++ b/solution.py
@@ -51,7 +51,10 @@
     weights = word_topic
     shares = topic_weight
     for step in range(ITERS):
-        row_phi = lax.all_gather(weights, "col", axis=0, tiled=True)
+        count = lax.axis_size("col")
+        pieces = jnp.stack([weights for _ in range(count)])
+        pieces = lax.all_to_all(pieces, "col", split_axis=0, concat_axis=0)
+        row_phi = jnp.concatenate(pieces, axis=0)
         col_phi = lax.all_gather(weights, "row", axis=0, tiled=True)
         scaled = (row_phi.astype(jnp.float32) * shares).astype(jnp.bfloat16)
         left_blocks = scaled.reshape(-1, BLK, K)

time: 1030 us -> 956 us (0.928)
  waiting for transfers between devices: 636 us -> 547 us
    all_gather x2 -> x0, waiting for transfers between devices: 96.7 us -> none  [local(): row_phi = lax.all_gather(weights, 'col', axis=0, tiled=True)]
    all_to_all x0 -> x2, waiting for transfers between devices: none -> 58.7 us  [local(): pieces = lax.all_to_all(pieces, 'col', split_axis=0, concat_axis=0)]
    all_gather x2, waiting for transfers between devices: 116 us -> 66.4 us  [local(): col_phi = lax.all_gather(weights, 'row', axis=0, tiled=True)]
where the time goes in v1:
time: 956 us; the launch traced here: 952 us
  waiting for transfers between devices  547 us (57%)
  blocking collectives  131 us (14%)
  other arithmetic  117 us (12%)
  local copies, waits for them, and re-layouts  89.6 us (9%)
  matrix products  41.8 us (4%)
  between operations  14.8 us (2%)
  starting transfers between devices  10 us (1%)
    reduce_scatter x2, waiting for transfers between devices, local(): lax.psum_scatter(col_terms, 'row', scatter_dimension=0, tiled=True)  213 us
    reduce_scatter x2, waiting for transfers between devices, local(): lax.psum_scatter(row_terms, 'col', scatter_dimension=0, tiled=True)  207 us
    psum x2, blocking collectives, local(): totals = lax.psum(jnp.sum(expected, axis=0), ('row', 'col'))  131 us
    all_gather x2, waiting for transfers between devices, local(): col_phi = lax.all_gather(weights, 'row', axis=0, tiled=True)  66.4 us
    all_to_all x2, waiting for transfers between devices, local(): pieces = lax.all_to_all(pieces, 'col', split_axis=0, concat_axis=0)  58.7 us
    scatter-add x14, other arithmetic, group_step(): results.append(carry[place].at[col_ids].add(col_part))  46.9 us
    scatter-add x14, other arithmetic, group_step(): results.append(carry[place].at[row_ids].add(row_part))  46.4 us
    gather x14, local copies, waits for them, and re-layouts, group_step(): right = right_blocks[col_ids]  39.7 us
  transfers between devices with their start and end apart: 8, of which 8 were waited for; matrix products, arithmetic and copies ran while one was open for 1% of the time, Pallas kernels for 0%

profile of v1, /device:TPU:1, one launch (start us, length us, event | category | flops | bytes accessed | tf_op | source)
XLA Modules:
  0.0 952.4 jit_solution(12244980892089200705)
XLA Ops:
  10.5 6.2 all-to-all-start
  17.4 29.8 %all-to-all-done = bf16[8,1024,128]{2,1,0:T(8,128)(2,1)S(1)} async-done(((bf16[8,1024,128]{2,1,0:T(8,128)(2,1)}), bf16[8,1024,128]{2,1,0:T(8,128)(2,1)S(1)}, u32[]{:S(2)}, u32[]{:S(2)}) %all-to-all-start) | async-done | bytes 2097184 | tf_op jit(solution)/shard_map/all_to_all | solution.py:56
  49.1 34.6 %all-gather.3.cloned.1.call-done = bf16[16384,128]{1,0:T(8,128)(2,1)} async-done(((bf16[1024,128]{1,0:T(8,128)(2,1)}), bf16[16384,128]{1,0:T(8,128)(2,1)}) %all-gather.3.cloned.1.call-update) | async-done | bytes 4194320 | tf_op jit(solution)/shard_map/all_gather | solution.py:58
  83.7 4.2 broadcast.74.clone
  90.4 108.6 %while.24 = (s32[]{:T(128)}, f32[32,256,128]{2,1,0:T(8,128)}, f32[64,256,128]{2,1,0:T(8,128)}, s32[]{:T(128)}, s32[64,2]{0,1:T(2,128)S(1)}, /*index=5*/s32[]{:T(...) while((s32[]{:T(128)}, f32[32,256,128]{2,1,0:T(8,128)}, ...), condition=%wide.region_3.4_spmd, body=%wide.region_0.3_spmd.sunk | while | flops 405276736 | bytes 17835532 | solution.py:44
  98.8 3.4 scatter_fusion.1
  102.7 3.3 scatter_fusion
  114.5 3.3 scatter_fusion.1
  133.7 3.3 scatter_fusion
  145.4 3.4 scatter_fusion.1
  176.4 3.4 scatter_fusion.1
  191.9 3.4 scatter_fusion.1
  195.7 3.4 scatter_fusion
  199.9 103.4 %reduce-scatter.5.cloned.1.call-done = f32[1024,128]{1,0:T(8,128)} async-done(((f32[8192,128]{1,0:T(8,128)}), f32[1024,128]{1,0:T(8,128)}) %reduce-scatter.5.cloned.1.call-update) | async-done | bytes 524304 | tf_op jit(solution)/shard_map/reduce_scatter | solution.py:65
  303.2 106.7 %reduce-scatter.7.cloned.1.call-done = f32[1024,128]{1,0:T(8,128)} async-done(((f32[16384,128]{1,0:T(8,128)}), f32[1024,128]{1,0:T(8,128)}) %reduce-scatter.7.cloned.1.call-update) | async-done | bytes 524304 | tf_op jit(solution)/shard_map/reduce_scatter | solution.py:66
  411.3 65.5 %psum.14 = f32[128]{0:T(128)S(1)} all-reduce(f32[128]{0:T(128)S(1)} %fusion.6), channel_id=1, replica_groups=mesh['row'=16,'col'=8] {'row','col'}, use_global_device_ids=true, to_apply=%region_7.8 | all-reduce | flops 128 | bytes 1024 | tf_op jit(solution)/shard_map/psum | solution.py:68
  481.4 3.6 all-to-all-start.1
  486.3 28.9 %all-to-all-done.1 = bf16[8,1024,128]{2,1,0:T(8,128)(2,1)S(1)} async-done(((bf16[8,1024,128]{2,1,0:T(8,128)(2,1)}), bf16[8,1024,128]{2,1,0:T(8,128)(2,1)S(1)}, u32[]{:S(2)}, u32[]{:S(2)}) %all-to-all-start.1) | async-done | bytes 2097184 | tf_op jit(solution)/shard_map/all_to_all | solution.py:56
  517.1 31.8 %all-gather.5.cloned.1.call-done = bf16[16384,128]{1,0:T(8,128)(2,1)} async-done(((bf16[1024,128]{1,0:T(8,128)(2,1)}), bf16[16384,128]{1,0:T(8,128)(2,1)}) %all-gather.5.cloned.1.call-update) | async-done | bytes 4194320 | tf_op jit(solution)/shard_map/all_gather | solution.py:58
  548.9 4.2 broadcast.74
  555.6 108.6 %while.25 = (s32[]{:T(128)}, f32[32,256,128]{2,1,0:T(8,128)}, f32[64,256,128]{2,1,0:T(8,128)}, s32[]{:T(128)}, s32[64,2]{0,1:T(2,128)S(1)}, /*index=5*/s32[]{:T(...) while((s32[]{:T(128)}, f32[32,256,128]{2,1,0:T(8,128)}, ...), condition=%wide.region_12.13_spmd, body=%wide.region_9.12_spmd.sunk | while | flops 405276736 | bytes 17835532 | solution.py:44
  564.0 3.4 scatter_fusion.3
  567.9 3.3 scatter_fusion.2
  579.6 3.3 scatter_fusion.3
  598.9 3.3 scatter_fusion.2
  610.6 3.4 scatter_fusion.3
  641.6 3.4 scatter_fusion.3
  657.1 3.4 scatter_fusion.3
  660.9 3.4 scatter_fusion.2
  664.8 103.6 %reduce-scatter.9.cloned.1.call-done = f32[1024,128]{1,0:T(8,128)} async-done(((f32[8192,128]{1,0:T(8,128)}), f32[1024,128]{1,0:T(8,128)}) %reduce-scatter.9.cloned.1.call-update) | async-done | bytes 524304 | tf_op jit(solution)/shard_map/reduce_scatter | solution.py:65
  768.4 106.7 %reduce-scatter.11.cloned.1.call-done = f32[1024,128]{1,0:T(8,128)} async-done(((f32[16384,128]{1,0:T(8,128)}), f32[1024,128]{1,0:T(8,128)}) %reduce-scatter.11.cloned.1.call-update) | async-done | bytes 524304 | tf_op jit(solution)/shard_map/reduce_scatter | solution.py:66
  876.5 65.3 %psum.15 = f32[128]{0:T(128)S(1)} all-reduce(f32[128]{0:T(128)S(1)} %fusion.7), channel_id=1, replica_groups=mesh['row'=16,'col'=8] {'row','col'}, use_global_device_ids=true, to_apply=%region_16.17 | all-reduce | flops 128 | bytes 1024 | tf_op jit(solution)/shard_map/psum | solution.py:68
  (186 shorter events, 188.5 us)
Async XLA Ops:
  7.2 40.0 %copy-start.3 = (f32[128]{0:T(128)S(1)}, f32[128]{0:T(128)}, u32[]{:S(2)}) copy-start(f32[128]{0:T(128)} %param.10) | copy-start | bytes 1540
  7.2 76.5 %all-gather.3.cloned.1.call-start = ((), (), s32[]{:S(2)}) async-start(), calls=%async_computation.6 | async-start | bytes 4456448 | tf_op jit(solution)/shard_map/all_gather | solution.py:58
  10.5 36.7 %all-to-all-start = ((bf16[8,1024,128]{2,1,0:T(8,128)(2,1)}), bf16[8,1024,128]{2,1,0:T(8,128)(2,1)S(1)}, u32[]{:S(2)}, u32[]{:S(2)}) async-start(bf16[8,1024,128]{2,1,0:T(8,128)(2,1)} %stack.4), calls=%async_computation | async-start | bytes 4194304 | tf_op jit(solution)/shard_map/all_to_all | solution.py:56
  16.7 286.5 %reduce-scatter.5.cloned.1.call-start = ((), (), s32[]{:S(2)}) async-start(), calls=%async_computation.7 | async-start | bytes 4718592 | tf_op jit(solution)/shard_map/reduce_scatter | solution.py:65
  88.0 2.5 copy-start.2
  199.1 210.8 %reduce-scatter.7.cloned.1.call-start = ((), (), s32[]{:S(2)}) async-start(), calls=%async_computation.8 | async-start | bytes 8912896 | tf_op jit(solution)/shard_map/reduce_scatter | solution.py:66
  199.1 210.8 %copy-start.1 = (bf16[1024,128]{1,0:T(8,128)(2,1)S(1)}, bf16[1024,128]{1,0:T(8,128)(2,1)}, u32[]{:S(2)}) copy-start(bf16[1024,128]{1,0:T(8,128)(2,1)} %param.9) | copy-start | bytes 786436
  199.8 349.1 %all-gather.5.cloned.1.call-start = ((), (), s32[]{:S(2)}) async-start(), calls=%async_computation.9 | async-start | bytes 4456448 | tf_op jit(solution)/shard_map/all_gather | solution.py:58
  481.4 33.8 %all-to-all-start.1 = ((bf16[8,1024,128]{2,1,0:T(8,128)(2,1)}), bf16[8,1024,128]{2,1,0:T(8,128)(2,1)S(1)}, u32[]{:S(2)}, u32[]{:S(2)}) async-start(bf16[8,1024,128]{2,1,0:T(8,128)(2,1)} %stack.5), calls=%async_computation.3 | async-start | bytes 4194304 | tf_op jit(solution)/shard_map/all_to_all | solution.py:56
  485.0 283.4 %reduce-scatter.9.cloned.1.call-start = ((), (), s32[]{:S(2)}) async-start(), calls=%async_computation.10 | async-start | bytes 4718592 | tf_op jit(solution)/shard_map/reduce_scatter | solution.py:65
  664.3 210.9 %reduce-scatter.11.cloned.1.call-start = ((), (), s32[]{:S(2)}) async-start(), calls=%async_computation.11 | async-start | bytes 8912896 | tf_op jit(solution)/shard_map/reduce_scatter | solution.py:66
  664.3 210.8 %copy-start = (bf16[1024,128]{1,0:T(8,128)(2,1)S(1)}, bf16[1024,128]{1,0:T(8,128)(2,1)}, u32[]{:S(2)}) copy-start(bf16[1024,128]{1,0:T(8,128)(2,1)} %divide_convert_fusion.1) | copy-start | bytes 786436
Sparse Core Ops, SparseCore 0:
  10.4 73.2 all-gather.2
  199.2 103.9 reduce-scatter.4
  307.6 102.2 reduce-scatter.6
  478.9 69.9 all-gather.4
  664.4 103.9 reduce-scatter.8
  772.6 102.5 reduce-scatter.10
